TPU v7x, 256 devices: a whole 4x4x8 slice. The times are simulated.
256 devices in a mesh: grp: 8 (over z_hi, core), blk: 32 (over x, y, z_lo).
Axes of the slice: x: 4, y: 4, z: 8 (z_hi: 4, z_lo: 2; z = z_hi * 2 + z_lo), core: 2. Of those that a mesh axis runs over, the one named last changes fastest.
Arguments:
- factors: bfloat16 [1024, 512, 512], P(('grp', 'blk')), may hold values from -6 to 6
- loadings: bfloat16 [512, 2048], replicated, may hold values from -0.25 to 0.25
- netload_map: bfloat16 [512, 200], replicated, may hold values from -0.25 to 0.25
- rule_weights: bfloat16 [32, 2048, 200], P('blk'), may hold values from -0.125 to 0.125
- rule_bias: float32 [32, 200], P('blk'), may hold values from -3 to 3
Outputs:
- decisions: bfloat16 [512, 1024, 200], P('blk', 'grp')
- rule_grad: float32 [32, 2048, 200], P('blk', 'grp')
All inputs are finite; a program needn't handle non-finite values.
Results may differ from a plain program's by a relative error of at most 0.01.
Values may be sent and summed in bfloat16 or wider, within the bound.
A program may use at most 128 MiB of HBM per device.

v0:
```python
import math
import jax
import jax.numpy as jnp
from jax import lax
from jax.sharding import PartitionSpec as P


def body(factors, loadings, netload_map, rule_weights, rule_bias):
    blocks = lax.axis_size("blk")
    groups = lax.axis_size("grp")
    path_dev, hours, width_k = factors.shape
    hour_blk = hours // blocks
    row_scale = 1.0 / math.sqrt(groups * blocks * path_dev * hour_blk)
    weights = rule_weights[0]
    offsets = rule_bias[0]
    ordered = jnp.transpose(factors.reshape(path_dev, blocks, hour_blk, width_k), (1, 2, 0, 3))
    features = jnp.tanh(
        jnp.einsum("...c,cf->...f", ordered, loadings, preferred_element_type=jnp.float32)
    ).astype(jnp.bfloat16)
    net_load = jnp.einsum(
        "...c,cd->...d", ordered, netload_map, preferred_element_type=jnp.float32
    ).astype(jnp.bfloat16)
    features, net_load = (features, net_load)
    decide_features = lax.all_to_all(features, "blk", split_axis=0, concat_axis=2, tiled=True)[0]
    decide_net_load = lax.all_to_all(net_load, "blk", split_axis=0, concat_axis=2, tiled=True)[0]
    dispatch = (
        jnp.einsum("krf,fd->krd", decide_features, weights, preferred_element_type=jnp.float32)
        + offsets
    )
    shortfall = decide_net_load.astype(jnp.float32) - dispatch
    slopes = (
        -4.0 * jax.nn.sigmoid(shortfall) + jax.nn.sigmoid(-shortfall) + 0.25 * dispatch
    ).astype(jnp.bfloat16)
    decisions, slopes, received = (dispatch.astype(jnp.bfloat16), slopes, decide_features)
    partial_grad = (
        jnp.einsum("krf,krd->fd", received, slopes, preferred_element_type=jnp.float32) * row_scale
    )[None]
    summed = lax.psum(partial_grad.astype(jnp.bfloat16), "grp").astype(jnp.float32)
    owned = partial_grad.shape[1] // groups
    grad_share = lax.dynamic_slice_in_dim(summed, lax.axis_index("grp") * owned, owned, 1)
    return (decisions, grad_share)


def solution(mesh):
    return jax.shard_map(
        body,
        mesh=mesh,
        in_specs=(P(("grp", "blk"), None, None), P(), P(), P("blk", None, None), P("blk", None)),
        out_specs=(P("blk", "grp", None), P("blk", "grp", None)),
        check_vma=False,
    )
```

profile of v0, /device:TPU:1, one launch (start us, length us, event | category | flops | bytes accessed | tf_op | source)
XLA Modules:
  0.0 289.5 jit_solution(17951146941334778530)
XLA Ops:
  7.2 0.0 copy-start
  7.2 3.4 %fusion.9 = bf16[32,16,4,200]{3,1,2,0:T(8,128)(2,1)} fusion(bf16[4,32,16,512]{3,2,1,0:T(8,128)(2,1)} %bitcast.49, bf16[512,200]{0,1:T(8,128)(2,1)} %param.7), kind=kOutput, calls=%fused_computation.13 | convolution fusion | flops 419840000 | bytes 3121152 | tf_op jit(solution)/shard_map/...c,cd->...d/dot_general | solution.py:20
  10.6 9.2 %all-to-all-start.1 = ((bf16[32,16,4,200]{3,1,2,0:T(8,128)(2,1)}), bf16[32,16,4,200]{3,1,2,0:T(8,128)(2,1)S(1)}, u32[]{:S(2)}, u32[]{:S(2)}) async-start(bf16[32,16,4,200]{3,1,2,0:T(8,128)(2,1)} %fusion.9), calls=%async_computation.1 | async-start | bytes 2097152 | tf_op jit(solution)/shard_map/all_to_all | solution.py:25
  19.8 0.0 copy-done
  19.8 8.3 %tanh_convert_fusion = bf16[32,16,4,2048]{3,1,2,0:T(8,128)(2,1)} fusion(bf16[512,2048]{1,0:T(8,128)(2,1)S(1)} %copy-done, bf16[4,32,16,512]{3,2,1,0:T(8,128)(2,1)} %bitcast.50), kind=kOutput, calls=%fused_computation | convolution fusion | flops 4299161600 | bytes 12582912 | tf_op jit(solution)/shard_map/...c,cf->...f/dot_general | solution.py:18
  28.2 8.4 %all-to-all-done.1 = bf16[32,16,4,200]{3,1,2,0:T(8,128)(2,1)S(1)} async-done(((bf16[32,16,4,200]{3,1,2,0:T(8,128)(2,1)}), bf16[32,16,4,200]{3,1,2,0:T(8,128)(2,1)S(1)}, u32[]{:S(2)}, u32[]{:S(2)}) %all-to-all-start.1) | async-done | bytes 819232 | tf_op jit(solution)/shard_map/all_to_all | solution.py:25
  36.6 5.0 %all-to-all-start = ((bf16[32,16,4,2048]{3,1,2,0:T(8,128)(2,1)}), bf16[32,16,4,2048]{3,1,2,0:T(8,128)(2,1)}, u32[]{:S(2)}, u32[]{:S(2)}) async-start(bf16[32,16,4,2048]{3,1,2,0:T(8,128)(2,1)} %tanh_convert_fusion), calls=%async_computation | async-start | bytes 16777216 | tf_op jit(solution)/shard_map/all_to_all | solution.py:24
  41.5 0.0 all-reduce.2.cloned.1.call-start
  41.6 1.6 bitcast_convert_fusion
  43.2 0.0 copy-start.2
  43.2 2.9 %copy.13 = f32[16,128,200]{1,2,0:T(8,128)} copy(f32[16,128,200]{2,0,1:T(8,128)} %bitcast.47) | data formatting | bytes 3276800 | tf_op jit(solution)/shard_map/convert_element_type | solution.py:30
  46.2 129.4 %all-to-all-done = bf16[32,16,4,2048]{3,1,2,0:T(8,128)(2,1)} async-done(((bf16[32,16,4,2048]{3,1,2,0:T(8,128)(2,1)}), bf16[32,16,4,2048]{3,1,2,0:T(8,128)(2,1)}, u32[]{:S(2)}, u32[]{:S(2)}) %all-to-all-start) | async-done | bytes 8388640 | tf_op jit(solution)/shard_map/all_to_all | solution.py:24
  175.6 0.0 copy-done.2
  175.6 7.1 %fusion.12 = f32[16,128,200]{2,0,1:T(8,128)} fusion(bf16[16,128,2048]{2,0,1:T(8,128)(2,1)} %bitcast.6, bf16[1,2048,200]{1,2,0:T(8,128)(2,1)S(1)} %copy-done.2), kind=kOutput, calls=%fused_computation.15 | convolution fusion | flops 1677721600 | bytes 10846208 | tf_op jit(solution)/shard_map/krf,fd->krd/dot_general | solution.py:27
  182.7 0.0 copy-start.1
  182.7 2.9 copy.17
  185.6 0.0 copy-done.1
  185.6 3.7 %add_convert_fusion = (bf16[16,128,200]{1,2,0:T(8,128)(2,1)S(1)}, bf16[16,128,200]{1,2,0:T(8,128)(2,1)}) fusion(f32[16,128,200]{1,2,0:T(8,128)} %copy.13, f32[16,128,200]{1,2,0:T(8,128)} %copy.17, f32[200]{0:T(256)S(1)} %bitcast.48), kind=kLoop, calls=%fused_computation.11 | loop fusion | flops 5324800 | bytes 4916000 | tf_op jit(solution)/shard_map/convert_element_type | solution.py:33
  189.3 1.7 copy.20
  191.0 6.4 %fusion.2 = bf16[1,2048,200]{1,2,0:T(8,128)(2,1)} fusion(bf16[16,128,2048]{2,0,1:T(8,128)(2,1)} %bitcast.6, bf16[16,128,200]{2,0,1:T(8,128)(2,1)} %copy.20), kind=kOutput, calls=%fused_computation.4 | convolution fusion | flops 1678540800 | bytes 10027008 | tf_op jit(solution)/shard_map/krf,krd->fd/dot_general | solution.py:36
  197.4 0.0 all-reduce.2.cloned.1.call-update
  197.4 83.7 %all-reduce.2.cloned.1.call-done = bf16[1,2048,200]{1,2,0:T(8,128)(2,1)} async-done(((bf16[1,2048,200]{1,2,0:T(8,128)(2,1)}), bf16[1,2048,200]{1,2,0:T(8,128)(2,1)}) %all-reduce.2.cloned.1.call-update) | async-done | bytes 819216 | tf_op jit(solution)/shard_map/psum | solution.py:38
  281.1 1.6 dynamic-slice_convert_fusion
Async XLA Ops:
  7.2 12.7 %copy-start = (bf16[512,2048]{1,0:T(8,128)(2,1)S(1)}, bf16[512,2048]{1,0:T(8,128)(2,1)}, u32[]{:S(2)}) copy-start(bf16[512,2048]{1,0:T(8,128)(2,1)} %param.6) | copy-start | bytes 6291460
  10.6 25.9 %all-to-all-start.1 = ((bf16[32,16,4,200]{3,1,2,0:T(8,128)(2,1)}), bf16[32,16,4,200]{3,1,2,0:T(8,128)(2,1)S(1)}, u32[]{:S(2)}, u32[]{:S(2)}) async-start(bf16[32,16,4,200]{3,1,2,0:T(8,128)(2,1)} %fusion.9), calls=%async_computation.1 | async-start | bytes 2097152 | tf_op jit(solution)/shard_map/all_to_all | solution.py:25
  36.6 139.0 %all-to-all-start = ((bf16[32,16,4,2048]{3,1,2,0:T(8,128)(2,1)}), bf16[32,16,4,2048]{3,1,2,0:T(8,128)(2,1)}, u32[]{:S(2)}, u32[]{:S(2)}) async-start(bf16[32,16,4,2048]{3,1,2,0:T(8,128)(2,1)} %tanh_convert_fusion), calls=%async_computation | async-start | bytes 16777216 | tf_op jit(solution)/shard_map/all_to_all | solution.py:24
  41.5 239.6 %all-reduce.2.cloned.1.call-start = ((), (), s32[]{:S(2)}) async-start(), calls=%async_computation.2 | async-start | bytes 1638400 | tf_op jit(solution)/shard_map/psum | solution.py:38
  43.2 132.4 %copy-start.2 = (bf16[1,2048,200]{1,2,0:T(8,128)(2,1)S(1)}, bf16[1,2048,200]{1,2,0:T(8,128)(2,1)}, u32[]{:S(2)}) copy-start(bf16[1,2048,200]{1,2,0:T(8,128)(2,1)} %param.8) | copy-start | bytes 2457604
  182.7 2.9 copy-start.1
Sparse Core Ops, SparseCore 0:
  197.5 83.5 all-reduce.1
where the time goes:
time: 290 us
  waiting for transfers between devices  222 us (77%)
  matrix products  25.3 us (9%)
  starting transfers between devices  14.2 us (5%)
  between operations  14.1 us (5%)
  local copies, waits for them, and re-layouts  7.5 us (3%)
  other arithmetic  6.93 us (2%)
    all_to_all x1, waiting for transfers between devices, body(): lax.all_to_all(features, 'blk', split_axis=0, concat_axis=2, tiled=True)[0]  129 us
    psum x1, waiting for transfers between devices, body(): lax.psum(partial_grad.astype(jnp.bfloat16), 'grp').astype(jnp.float32)  83.7 us
    all_to_all x1, starting transfers between devices, body(): lax.all_to_all(net_load, 'blk', split_axis=0, concat_axis=2, tiled=True)[0]  9.21 us
    all_to_all x1, waiting for transfers between devices, body(): lax.all_to_all(net_load, 'blk', split_axis=0, concat_axis=2, tiled=True)[0]  8.41 us
    dot_general x1, matrix products, body(): jnp.einsum('...c,cf->...f', ordered, loadings, preferred_element_type=jnp...  8.32 us
    dot_general x1, matrix products, body(): jnp.einsum('krf,fd->krd', decide_features, weights, preferred_element_typ...  7.12 us
    dot_general x1, matrix products, body(): jnp.einsum('krf,krd->fd', received, slopes, preferred_element_type=jnp.fl...  6.41 us
  transfers between devices with their start and end apart: 3, of which 3 were waited for; matrix products, arithmetic and copies ran while one was open for 4% of the time, Pallas kernels for 0%

commit v1 on v0

--- a/solution.py
+++ b/solution.py
@@ -35,7 +35,9 @@
     partial_grad = (
         jnp.einsum("krf,krd->fd", received, slopes, preferred_element_type=jnp.float32) * row_scale
     )[None]
-    summed = lax.psum(partial_grad.astype(jnp.bfloat16), "grp").astype(jnp.float32)
+    summed = jnp.sum(lax.all_gather(partial_grad.astype(jnp.bfloat16), "grp"), axis=0).astype(
+        jnp.float32
+    )
     owned = partial_grad.shape[1] // groups
     grad_share = lax.dynamic_slice_in_dim(summed, lax.axis_index("grp") * owned, owned, 1)
     return (decisions, grad_share)

time: 290 us -> 300 us (1.034)
  local copies, waits for them, and re-layouts: 7.5 us -> 14.9 us
  other arithmetic: 6.93 us -> 11.8 us
  waiting for transfers between devices: 222 us -> 219 us
    psum x1 -> x0, waiting for transfers between devices: 83.7 us -> none  [body(): lax.psum(partial_grad.astype(jnp.bfloat16), 'grp').astype(jnp.float32)]
    all_gather x0 -> x1, waiting for transfers between devices: none -> 81.2 us  [body(): lax.all_gather(partial_grad.astype(jnp.bfloat16), 'grp')]
    unnamed x6 -> x7, local copies, waits for them, and re-layouts: 0.02 us -> 7.39 us
    reduce_sum x0 -> x1, other arithmetic: none -> 5.73 us  [body(): jnp.sum(lax.all_gather(partial_grad.astype(jnp.bfloat16), 'grp'), axis=0)]
where the time goes in v1:
time: 300 us; the launch traced here: 299 us
  waiting for transfers between devices  219 us (73%)
  matrix products  25.3 us (8%)
  local copies, waits for them, and re-layouts  14.9 us (5%)
  starting transfers between devices  14.2 us (5%)
  between operations  14.1 us (5%)
  other arithmetic  11.8 us (4%)
    all_to_all x1, waiting for transfers between devices, body(): lax.all_to_all(features, 'blk', split_axis=0, concat_axis=2, tiled=True)[0]  129 us
    all_gather x1, waiting for transfers between devices, body(): lax.all_gather(partial_grad.astype(jnp.bfloat16), 'grp')  81.2 us
    all_to_all x1, starting transfers between devices, body(): lax.all_to_all(net_load, 'blk', split_axis=0, concat_axis=2, tiled=True)[0]  9.21 us
    all_to_all x1, waiting for transfers between devices, body(): lax.all_to_all(net_load, 'blk', split_axis=0, concat_axis=2, tiled=True)[0]  8.4 us
    dot_general x1, matrix products, body(): jnp.einsum('...c,cf->...f', ordered, loadings, preferred_element_type=jnp...  8.31 us
    unnamed x7, local copies, waits for them, and re-layouts  7.39 us
    dot_general x1, matrix products, body(): jnp.einsum('krf,fd->krd', decide_features, weights, preferred_element_typ...  7.12 us
    dot_general x1, matrix products, body(): jnp.einsum('krf,krd->fd', received, slopes, preferred_element_type=jnp.fl...  6.42 us
  transfers between devices with their start and end apart: 3, of which 3 were waited for; matrix products, arithmetic and copies ran while one was open for 4% of the time, Pallas kernels for 0%

profile of v1, /device:TPU:1, one launch (start us, length us, event | category | flops | bytes accessed | tf_op | source)
XLA Modules:
  0.0 299.2 jit_solution(1903493360762272389)
XLA Ops:
  7.2 0.0 copy-start
  7.2 3.4 %fusion.8 = bf16[32,16,4,200]{3,1,2,0:T(8,128)(2,1)} fusion(bf16[4,32,16,512]{3,2,1,0:T(8,128)(2,1)} %bitcast.53, bf16[512,200]{0,1:T(8,128)(2,1)} %param.7), kind=kOutput, calls=%fused_computation.13 | convolution fusion | flops 419840000 | bytes 3121152 | tf_op jit(solution)/shard_map/...c,cd->...d/dot_general | solution.py:20
  10.6 9.2 %all-to-all-start.1 = ((bf16[32,16,4,200]{3,1,2,0:T(8,128)(2,1)}), bf16[32,16,4,200]{3,1,2,0:T(8,128)(2,1)S(1)}, u32[]{:S(2)}, u32[]{:S(2)}) async-start(bf16[32,16,4,200]{3,1,2,0:T(8,128)(2,1)} %fusion.8), calls=%async_computation.1 | async-start | bytes 2097152 | tf_op jit(solution)/shard_map/all_to_all | solution.py:25
  19.8 0.0 copy-done
  19.8 8.3 %tanh_convert_fusion = bf16[32,16,4,2048]{3,1,2,0:T(8,128)(2,1)} fusion(bf16[512,2048]{1,0:T(8,128)(2,1)S(1)} %copy-done, bf16[4,32,16,512]{3,2,1,0:T(8,128)(2,1)} %bitcast.54), kind=kOutput, calls=%fused_computation | convolution fusion | flops 4299161600 | bytes 12582912 | tf_op jit(solution)/shard_map/...c,cf->...f/dot_general | solution.py:18
  28.2 8.4 %all-to-all-done.1 = bf16[32,16,4,200]{3,1,2,0:T(8,128)(2,1)S(1)} async-done(((bf16[32,16,4,200]{3,1,2,0:T(8,128)(2,1)}), bf16[32,16,4,200]{3,1,2,0:T(8,128)(2,1)S(1)}, u32[]{:S(2)}, u32[]{:S(2)}) %all-to-all-start.1) | async-done | bytes 819232 | tf_op jit(solution)/shard_map/all_to_all | solution.py:25
  36.6 5.0 %all-to-all-start = ((bf16[32,16,4,2048]{3,1,2,0:T(8,128)(2,1)}), bf16[32,16,4,2048]{3,1,2,0:T(8,128)(2,1)}, u32[]{:S(2)}, u32[]{:S(2)}) async-start(bf16[32,16,4,2048]{3,1,2,0:T(8,128)(2,1)} %tanh_convert_fusion), calls=%async_computation | async-start | bytes 16777216 | tf_op jit(solution)/shard_map/all_to_all | solution.py:24
  41.5 0.0 all-gather.3.cloned.1.call-start
  41.6 1.6 bitcast_convert_fusion
  43.2 0.0 copy-start.2
  43.2 2.9 copy.13
  46.2 129.3 %all-to-all-done = bf16[32,16,4,2048]{3,1,2,0:T(8,128)(2,1)} async-done(((bf16[32,16,4,2048]{3,1,2,0:T(8,128)(2,1)}), bf16[32,16,4,2048]{3,1,2,0:T(8,128)(2,1)}, u32[]{:S(2)}, u32[]{:S(2)}) %all-to-all-start) | async-done | bytes 8388640 | tf_op jit(solution)/shard_map/all_to_all | solution.py:24
  175.5 0.0 copy-done.2
  175.5 7.1 %fusion.11 = f32[16,128,200]{2,0,1:T(8,128)} fusion(bf16[16,128,2048]{2,0,1:T(8,128)(2,1)} %bitcast.6, bf16[1,2048,200]{1,2,0:T(8,128)(2,1)S(1)} %copy-done.2), kind=kOutput, calls=%fused_computation.15 | convolution fusion | flops 1677721600 | bytes 10846208 | tf_op jit(solution)/shard_map/krf,fd->krd/dot_general | solution.py:27
  182.6 2.9 copy.17
  185.5 0.0 copy-done.1
  185.5 3.7 %add_convert_fusion = (bf16[16,128,200]{1,2,0:T(8,128)(2,1)S(1)}, bf16[16,128,200]{1,2,0:T(8,128)(2,1)}) fusion(f32[16,128,200]{1,2,0:T(8,128)} %copy.13, f32[16,128,200]{1,2,0:T(8,128)} %copy.17, f32[200]{0:T(256)S(1)} %bitcast.52), kind=kLoop, calls=%fused_computation.11 | loop fusion | flops 5324800 | bytes 4916000 | tf_op jit(solution)/shard_map/convert_element_type | solution.py:33
  189.2 1.7 copy.20
  190.9 6.4 %fusion.1 = bf16[2048,200]{0,1:T(8,128)(2,1)} fusion(bf16[16,128,2048]{2,0,1:T(8,128)(2,1)} %bitcast.6, bf16[16,128,200]{2,0,1:T(8,128)(2,1)} %copy.20), kind=kOutput, calls=%fused_computation.4 | convolution fusion | flops 1678540800 | bytes 10027008 | tf_op jit(solution)/shard_map/krf,krd->fd/dot_general | solution.py:36
  197.3 0.0 all-gather.3.cloned.1.call-update
  197.3 81.2 %all-gather.3.cloned.1.call-done = bf16[16384,200]{0,1:T(8,128)(2,1)} async-done(((bf16[2048,200]{0,1:T(8,128)(2,1)}), bf16[16384,200]{0,1:T(8,128)(2,1)}) %all-gather.3.cloned.1.call-update) | async-done | bytes 6553616 | tf_op jit(solution)/shard_map/all_gather | solution.py:38
  278.5 7.4 %copy.21 = bf16[25,8,8,2048]{3,2,1,0:T(8,128)(2,1)S(1)} copy(bf16[25,8,8,2048]{3,1,2,0:T(8,128)(2,1)} %bitcast.51) | data formatting | bytes 13107200
  285.9 5.7 %bitcast_reduce_fusion = bf16[2048,200]{0,1:T(8,128)(2,1)S(1)} fusion(bf16[25,8,8,2048]{3,2,1,0:T(8,128)(2,1)S(1)} %copy.21), kind=kLoop, calls=%fused_computation.1 | loop fusion | flops 2867200 | bytes 7372800 | tf_op jit(solution)/shard_map/reduce_sum | solution.py:38
  291.6 0.7 convert_bitcast_fusion
  (1 shorter events, 0.0 us)
Async XLA Ops:
  7.2 12.7 %copy-start = (bf16[512,2048]{1,0:T(8,128)(2,1)S(1)}, bf16[512,2048]{1,0:T(8,128)(2,1)}, u32[]{:S(2)}) copy-start(bf16[512,2048]{1,0:T(8,128)(2,1)} %param.6) | copy-start | bytes 6291460
  10.6 25.9 %all-to-all-start.1 = ((bf16[32,16,4,200]{3,1,2,0:T(8,128)(2,1)}), bf16[32,16,4,200]{3,1,2,0:T(8,128)(2,1)S(1)}, u32[]{:S(2)}, u32[]{:S(2)}) async-start(bf16[32,16,4,200]{3,1,2,0:T(8,128)(2,1)} %fusion.8), calls=%async_computation.1 | async-start | bytes 2097152 | tf_op jit(solution)/shard_map/all_to_all | solution.py:25
  36.6 138.9 %all-to-all-start = ((bf16[32,16,4,2048]{3,1,2,0:T(8,128)(2,1)}), bf16[32,16,4,2048]{3,1,2,0:T(8,128)(2,1)}, u32[]{:S(2)}, u32[]{:S(2)}) async-start(bf16[32,16,4,2048]{3,1,2,0:T(8,128)(2,1)} %tanh_convert_fusion), calls=%async_computation | async-start | bytes 16777216 | tf_op jit(solution)/shard_map/all_to_all | solution.py:24
  41.5 237.0 %all-gather.3.cloned.1.call-start = ((), (), s32[]{:S(2)}) async-start(), calls=%async_computation.2 | async-start | bytes 7372800 | tf_op jit(solution)/shard_map/all_gather | solution.py:38
  43.2 132.3 %copy-start.2 = (bf16[1,2048,200]{1,2,0:T(8,128)(2,1)S(1)}, bf16[1,2048,200]{1,2,0:T(8,128)(2,1)}, u32[]{:S(2)}) copy-start(bf16[1,2048,200]{1,2,0:T(8,128)(2,1)} %param.8) | copy-start | bytes 2457604
  182.6 2.9 copy-start.1
Sparse Core Ops, SparseCore 0:
  197.4 81.0 all-gather.2
